TPU v7x, 32 devices: a whole 2x2x4 slice. The times are simulated.
32 devices in a mesh: tm: 8 (over y, x, core), sector: 4 (over z).
Axes of the slice: x: 2, y: 2, z: 4, core: 2. Of those that a mesh axis runs over, the one named last changes fastest.
Arguments:
- propagator: bfloat16 [4, 8, 640, 640], P('sector', 'tm'), may hold values from -6 to 6
- rising_op: bfloat16 [4, 640, 640], P('sector'), may hold values from -0.25 to 0.25
- energies: float32 [4, 640], P('sector'), may hold values from 0.5 to 40
- hyb_particle: float32 [8], P('tm'), may hold values from 0.2 to 1
- hyb_hole: float32 [8], P('tm'), may hold values from 0.2 to 1
- sector_sizes: int32 [4], P('sector'), may hold values from 160 to 640, as said below
Outputs:
- new_prop: bfloat16 [4, 8, 640, 640], P('sector', 'tm')
Inputs may be any that keep to these rules, and one draw needn't show every extreme that they name: `sector_sizes`: one sector holds exactly 640 states.
All inputs are finite; a program needn't handle non-finite values.
Results may differ from a plain program's by a relative error of at most 0.0061.
Values may be sent and summed in bfloat16 or wider, within the bound.
A program may use at most 128 MiB of HBM per device.

v0:
```python
import jax
import jax.numpy as jnp
from jax import lax
from jax.sharding import PartitionSpec as P


def shifted(block, axis, distance):
    devices = range(lax.axis_size(axis))
    route = [(i - distance, i) for i in devices if i - distance in devices]
    return lax.ppermute(block, axis, route)


def per_device(propagator, rising_op, energies, hyb_particle, hyb_hole, sector_sizes):
    t_dev = propagator.shape[1]
    states = propagator.shape[2]
    time_count = t_dev * lax.axis_size("tm")
    step_size = 1.0 / time_count
    positions = jnp.arange(states, dtype=jnp.int32)
    live_mask = positions < sector_sizes[0]
    square = live_mask[:, None] & live_mask[None, :]
    masked_prop = jnp.where(square[None], propagator[0], jnp.zeros((), jnp.bfloat16))
    operator = rising_op[0]
    raised = jnp.einsum(
        "ik,tkl->til", operator, masked_prop, preferred_element_type=jnp.float32
    ).astype(jnp.bfloat16)
    upward = jnp.einsum("tik,jk->tij", raised, operator, preferred_element_type=jnp.float32).astype(
        jnp.bfloat16
    )
    from_below = shifted(upward, "sector", 1)
    from_above = shifted(masked_prop, "sector", -1)
    lowered = jnp.einsum(
        "ki,tkl->til", operator, from_above, preferred_element_type=jnp.float32
    ).astype(jnp.bfloat16)
    downward = jnp.einsum("tik,kl->til", lowered, operator, preferred_element_type=jnp.float32)
    combined = (
        hyb_particle[:, None, None] * from_below.astype(jnp.float32)
        + hyb_hole[:, None, None] * downward
    )
    self_energy = jnp.where(square[None], combined, jnp.zeros((), jnp.float32)).astype(jnp.bfloat16)
    rows_each = states // lax.axis_size("tm")
    first_row = lax.axis_index("tm") * rows_each
    lag_rows = lax.all_to_all(self_energy, "tm", split_axis=1, concat_axis=0, tiled=True)
    history = lax.all_gather(masked_prop, "tm", axis=0, tiled=True)
    mirrored = jnp.concatenate([history[::-1], history], 0)
    slots = jnp.arange(time_count, dtype=jnp.int32)
    wide_slots = jnp.arange(time_count + 1, dtype=jnp.int32)

    def pair_step(lag, sums):
        forward, backward = sums
        other = time_count - 1 - lag
        window = lax.dynamic_slice_in_dim(mirrored, lag, time_count + 1, 0)
        near = lax.dynamic_index_in_dim(lag_rows, lag, 0, keepdims=False)
        far = lax.dynamic_index_in_dim(lag_rows, other, 0, keepdims=False)
        left = jnp.where((wide_slots < time_count - lag)[:, None, None], near[None], far[None])
        product = jnp.einsum("uik,ukl->uil", left, window, preferred_element_type=jnp.float32)
        backward = backward + jnp.where(
            (slots < time_count - lag)[:, None, None],
            product[:time_count],
            jnp.zeros((), jnp.float32),
        )
        forward = forward + jnp.where(
            (slots >= time_count - lag - 1)[:, None, None], product[1:], jnp.zeros((), jnp.float32)
        )
        return (forward, backward)

    empty_rows = jnp.zeros((time_count, rows_each, states), jnp.float32)
    forward, backward = lax.fori_loop(0, time_count // 2, pair_step, (empty_rows, empty_rows))
    convolved = step_size * (forward + backward[::-1])
    row_ids = first_row + jnp.arange(rows_each, dtype=jnp.int32)
    row_rates = lax.dynamic_slice_in_dim(energies[0], first_row, rows_each, 0)
    decay_rows = jnp.exp(-step_size * row_rates)

    def advance(running, term):
        running = decay_rows[:, None] * running + term
        return (running, running)

    _, summed = lax.scan(advance, jnp.zeros((rows_each, states), jnp.float32), convolved)
    moments = jnp.arange(time_count).astype(jnp.float32) * step_size
    live_rows = row_ids < sector_sizes[0]
    free_part = jnp.where(
        live_rows[None, :],
        jnp.exp(-row_rates[None, :] * moments[:, None]),
        jnp.zeros((), jnp.float32),
    )
    diagonal = jnp.where(
        (row_ids[:, None] == positions[None, :])[None],
        free_part[:, :, None],
        jnp.zeros((), jnp.float32),
    )
    new_rows = (diagonal - step_size * summed).astype(jnp.bfloat16)
    return lax.all_to_all(new_rows, "tm", split_axis=0, concat_axis=1, tiled=True)[None]


def solution(mesh):
    placed = (
        P("sector", "tm", None, None),
        P("sector", None, None),
        P("sector", None),
        P("tm"),
        P("tm"),
        P("sector"),
    )
    return jax.shard_map(
        per_device,
        mesh=mesh,
        in_specs=placed,
        out_specs=P("sector", "tm", None, None),
        check_vma=False,
    )
```

profile of v0, /device:TPU:0, one launch (start us, length us, event | category | flops | bytes accessed | tf_op | source)
XLA Modules:
  0.0 162.4 jit_solution(225361923420501898)
XLA Ops:
  7.3 2.4 %and_select_fusion.1 = bf16[1,640,640]{2,1,0:T(8,128)(2,1)} fusion(bf16[1,1,640,640]{3,2,1,0:T(8,128)(2,1)} %param.10, pred[640]{0:T(1024)(128)(4,1)S(1)} %iota_compare_fusion.4), kind=kLoop, calls=%fused_computation.23 | loop fusion | flops 819200 | bytes 1639040 | tf_op jit(solution)/shard_map/jit(_where)/select_n | solution.py:21
  9.7 0.0 all-gather.2.cloned.1.call-update
  9.7 1.3 collective-permute-start.1
  11.0 2.9 %fusion.15 = bf16[1,640,640]{2,1,0:T(8,128)(2,1)} fusion(bf16[1,1,640,640]{3,2,1,0:T(8,128)(2,1)S(1)} %copy-done.1, bf16[1,640,640]{2,1,0:T(8,128)(2,1)S(1)} %copy-done, pred[640]{0:T(1024)(128)(4,1)S(1)} %iota_compare_fusion.4), kind=kOutput, calls=%fused_computation.33 | convolution fusion | flops 1050214400 | bytes 2458240 | tf_op jit(solution)/shard_map/tik,jk->tij/dot_general | solution.py:26
  13.9 5.6 %collective-permute-start = (bf16[1,640,640]{2,1,0:T(8,128)(2,1)}, bf16[1,640,640]{2,1,0:T(8,128)(2,1)S(1)}, u32[]{:S(2)}, u32[]{:S(2)}) collective-permute-start(bf16[1,640,640]{2,1,0:T(8,128)(2,1)} %fusion.15), channel_id=1, source_target_pairs={{0,1},{1,2},{2,3},{4,5},{5,6},{6,7},{8,9},{9,10},{10,11},{12,13},{... | collective-permute-start | bytes 2457608 | tf_op jit(solution)/shard_map/ppermute | solution.py:10
  20.9 12.3 %collective-permute-done.1 = bf16[1,640,640]{2,1,0:T(8,128)(2,1)S(1)} collective-permute-done((bf16[1,640,640]{2,1,0:T(8,128)(2,1)}, bf16[1,640,640]{2,1,0:T(8,128)(2,1)S(1)}, u32[]{:S(2)}, u32[]{:S(2)}) %collective-permute-start.1) | collective-permute-done | bytes 819232 | tf_op jit(solution)/shard_map/ppermute | solution.py:10
  33.1 4.2 %collective-permute-done = bf16[1,640,640]{2,1,0:T(8,128)(2,1)S(1)} collective-permute-done((bf16[1,640,640]{2,1,0:T(8,128)(2,1)}, bf16[1,640,640]{2,1,0:T(8,128)(2,1)S(1)}, u32[]{:S(2)}, u32[]{:S(2)}) %collective-permute-start) | collective-permute-done | bytes 819232 | tf_op jit(solution)/shard_map/ppermute | solution.py:10
  37.3 3.7 %fusion.13 = bf16[1,640,640]{2,1,0:T(8,128)(2,1)S(1)} fusion(bf16[1,640,640]{2,1,0:T(8,128)(2,1)S(1)} %collective-permute-done, bf16[1,640,640]{2,1,0:T(8,128)(2,1)} %copy-done.2, bf16[1,640,640]{2,1,0:T(8,128)(2,1)S(1)} %copy-done, f32[]{:T(128)} %bitcast.66, f32[]{:T(128)} %bitcast.65, pred[640]{0:T(1024)(128)(4,1)S(1)} %iota_compare_fusion.4), kind=kOutput, calls=%fused_computation.24 | convolution fusion | flops 1051852800 | bytes 3277448 | tf_op jit(solution)/shard_map/tik,kl->til/dot_general | solution.py:34
  41.0 1.3 copy.11
  42.3 0.5 broadcast.254
  42.8 5.6 %reduce = bf16[640,640]{1,0:T(8,128)(2,1)S(1)} reduce(bf16[640,1,640]{2,1,0:T(2,128)(2,1)S(1)} %bitcast.69, bf16[]{:T(256)} %broadcast.254), dimensions={1}, to_apply=%bitcast.60.reduce_sub_computation | reduce | bytes 1638402
  48.4 1.1 reshape.286
  49.5 4.4 %all-to-all-start = ((bf16[8,2,25600]{2,1,0:T(2,128)(2,1)}), bf16[8,2,25600]{2,1,0:T(2,128)(2,1)}, u32[]{:S(2)}, u32[]{:S(2)}) async-start(bf16[8,2,25600]{2,1,0:T(2,128)(2,1)} %reshape.286), calls=%async_computation | async-start | bytes 1638400 | tf_op jit(solution)/shard_map/all_to_all | solution.py:42
  54.0 0.8 negate_bitcast_fusion
  54.8 0.1 exponential_select_fusion
  54.8 0.1 iota_compare_fusion.3
  54.9 12.1 %all-to-all-done = bf16[8,2,25600]{2,1,0:T(2,128)(2,1)} async-done(((bf16[8,2,25600]{2,1,0:T(2,128)(2,1)}), bf16[8,2,25600]{2,1,0:T(2,128)(2,1)}, u32[]{:S(2)}, u32[]{:S(2)}) %all-to-all-start) | async-done | bytes 819232 | tf_op jit(solution)/shard_map/all_to_all | solution.py:42
  67.1 4.0 %reshape.287 = bf16[640,1,640]{2,1,0:T(2,128)(2,1)S(1)} reshape(bf16[8,2,25600]{2,1,0:T(2,128)(2,1)} %all-to-all-done) | data formatting | bytes 1638400
  71.1 1.0 copy.9
  72.1 6.3 %rev.6 = bf16[8,640,640]{2,1,0:T(8,128)(2,1)} reverse(bf16[8,640,640]{2,1,0:T(8,128)(2,1)} %all-gather.2.cloned.1.call-done), dimensions={0} | reverse | bytes 13107200 | tf_op jit(solution)/shard_map/rev | solution.py:44
  78.5 12.3 %pad_maximum_fusion = bf16[16,640,640]{2,1,0:T(8,128)(2,1)} fusion(bf16[8,640,640]{2,1,0:T(8,128)(2,1)} %all-gather.2.cloned.1.call-done, bf16[8,640,640]{2,1,0:T(8,128)(2,1)} %rev.6), kind=kLoop, calls=%fused_computation.21 | loop fusion | flops 6553600 | bytes 26214400 | tf_op jit(solution)/shard_map/concatenate | solution.py:44
  90.8 36.5 %while.35 = (s32[]{:T(128)}, f32[8,80,640]{2,1,0:T(8,128)}, f32[8,80,640]{2,1,0:T(8,128)}, bf16[8,80,640]{2,1,0:T(8,128)(2,1)}, bf16[16,640,640]{2,1,0:T(8,128)(...) while((s32[]{:T(128)}, f32[8,80,640]{2,1,0:T(8,128)}, ...), condition=%wide.region_1.2_spmd.clone.clone, body=%wide.region_0.1_spmd.clone.clone.sunk | while | flops 592742400 | bytes 19661552 | solution.py:67
  90.8 1.0 dynamic-slice_bitcast_fusion.3
  91.8 4.6 %fusion.40 = f32[9,80,640]{2,1,0:T(8,128)S(1)} fusion(bf16[16,640,640]{2,1,0:T(8,128)(2,1)} %get-tuple-element.458, s32[]{:T(128)} %get-tuple-element.444, pred[9]{0:T(512)(128)(4,1)S(1)} %iota_compare_fusion.7, bf16[80,640]{1,0:T(8,128)(2,1)S(1)} %get-tuple-element.428, bf16[80,640]{1,0:T(8,128)(2,1)S(1)} %get-tuple-element.429), kind=kOutput, calls=%fused_computation.5.clone.1 | convolution fusion | flops 590284800 | bytes 9421321 | tf_op jit(solution)/shard_map/while/body/eval_jaxpr/uik,ukl->uil/dot_general | solution.py:55
  96.4 2.1 %fusion.41 = (f32[8,80,640]{2,1,0:T(8,128)}, f32[8,80,640]{2,1,0:T(8,128)}) fusion(f32[9,80,640]{2,1,0:T(8,128)S(1)} %fusion.40, f32[8,80,640]{2,1,0:T(8,128)} %get-tuple-element.446, pred[8]{0:T(512)(128)(4,1)S(1)} %get-tuple-element.430, pred[]{:T(512)S(6)} %compare.7, pred[8]{0:T(512)(128)(4,1)S(1)} %get-tuple-element.431, ...), kind=kLoop, calls=%fused_computation.8.clone.1 | loop fusion | flops 2457600 | bytes 9830417 | tf_op jit(solution)/shard_map/while/body/eval_jaxpr/add | solution.py:56
  98.5 1.0 dynamic-slice_bitcast_fusion.3
  99.5 4.6 %fusion.40 = f32[9,80,640]{2,1,0:T(8,128)S(1)} fusion(bf16[16,640,640]{2,1,0:T(8,128)(2,1)} %get-tuple-element.458, s32[]{:T(128)} %get-tuple-element.444, pred[9]{0:T(512)(128)(4,1)S(1)} %iota_compare_fusion.7, bf16[80,640]{1,0:T(8,128)(2,1)S(1)} %get-tuple-element.428, bf16[80,640]{1,0:T(8,128)(2,1)S(1)} %get-tuple-element.429), kind=kOutput, calls=%fused_computation.5.clone.1 | convolution fusion | flops 590284800 | bytes 9421321 | tf_op jit(solution)/shard_map/while/body/eval_jaxpr/uik,ukl->uil/dot_general | solution.py:55
  104.1 4.0 %fusion.41 = (f32[8,80,640]{2,1,0:T(8,128)}, f32[8,80,640]{2,1,0:T(8,128)}) fusion(f32[9,80,640]{2,1,0:T(8,128)S(1)} %fusion.40, f32[8,80,640]{2,1,0:T(8,128)} %get-tuple-element.446, pred[8]{0:T(512)(128)(4,1)S(1)} %get-tuple-element.430, pred[]{:T(512)S(6)} %compare.7, pred[8]{0:T(512)(128)(4,1)S(1)} %get-tuple-element.431, ...), kind=kLoop, calls=%fused_computation.8.clone.1 | loop fusion | flops 2457600 | bytes 9830417 | tf_op jit(solution)/shard_map/while/body/eval_jaxpr/add | solution.py:56
  108.1 1.0 dynamic-slice_bitcast_fusion.3
  109.1 4.6 %fusion.40 = f32[9,80,640]{2,1,0:T(8,128)S(1)} fusion(bf16[16,640,640]{2,1,0:T(8,128)(2,1)} %get-tuple-element.458, s32[]{:T(128)} %get-tuple-element.444, pred[9]{0:T(512)(128)(4,1)S(1)} %iota_compare_fusion.7, bf16[80,640]{1,0:T(8,128)(2,1)S(1)} %get-tuple-element.428, bf16[80,640]{1,0:T(8,128)(2,1)S(1)} %get-tuple-element.429), kind=kOutput, calls=%fused_computation.5.clone.1 | convolution fusion | flops 590284800 | bytes 9421321 | tf_op jit(solution)/shard_map/while/body/eval_jaxpr/uik,ukl->uil/dot_general | solution.py:55
  113.7 4.0 %fusion.41 = (f32[8,80,640]{2,1,0:T(8,128)}, f32[8,80,640]{2,1,0:T(8,128)}) fusion(f32[9,80,640]{2,1,0:T(8,128)S(1)} %fusion.40, f32[8,80,640]{2,1,0:T(8,128)} %get-tuple-element.446, pred[8]{0:T(512)(128)(4,1)S(1)} %get-tuple-element.430, pred[]{:T(512)S(6)} %compare.7, pred[8]{0:T(512)(128)(4,1)S(1)} %get-tuple-element.431, ...), kind=kLoop, calls=%fused_computation.8.clone.1 | loop fusion | flops 2457600 | bytes 9830417 | tf_op jit(solution)/shard_map/while/body/eval_jaxpr/add | solution.py:56
  117.7 1.0 dynamic-slice_bitcast_fusion.3
  118.7 4.6 %fusion.40 = f32[9,80,640]{2,1,0:T(8,128)S(1)} fusion(bf16[16,640,640]{2,1,0:T(8,128)(2,1)} %get-tuple-element.458, s32[]{:T(128)} %get-tuple-element.444, pred[9]{0:T(512)(128)(4,1)S(1)} %iota_compare_fusion.7, bf16[80,640]{1,0:T(8,128)(2,1)S(1)} %get-tuple-element.428, bf16[80,640]{1,0:T(8,128)(2,1)S(1)} %get-tuple-element.429), kind=kOutput, calls=%fused_computation.5.clone.1 | convolution fusion | flops 590284800 | bytes 9421321 | tf_op jit(solution)/shard_map/while/body/eval_jaxpr/uik,ukl->uil/dot_general | solution.py:55
  123.3 4.0 %fusion.41 = (f32[8,80,640]{2,1,0:T(8,128)}, f32[8,80,640]{2,1,0:T(8,128)}) fusion(f32[9,80,640]{2,1,0:T(8,128)S(1)} %fusion.40, f32[8,80,640]{2,1,0:T(8,128)} %get-tuple-element.446, pred[8]{0:T(512)(128)(4,1)S(1)} %get-tuple-element.430, pred[]{:T(512)S(6)} %compare.7, pred[8]{0:T(512)(128)(4,1)S(1)} %get-tuple-element.431, ...), kind=kLoop, calls=%fused_computation.8.clone.1 | loop fusion | flops 2457600 | bytes 9830417 | tf_op jit(solution)/shard_map/while/body/eval_jaxpr/add | solution.py:56
  127.3 3.3 %add_multiply_fusion = f32[8,80,640]{2,1,0:T(8,128)} fusion(f32[8,80,640]{2,1,0:T(8,128)} %get-tuple-element.265, f32[8,80,640]{2,1,0:T(8,128)} %get-tuple-element.266), kind=kLoop, calls=%fused_computation.27 | loop fusion | flops 819200 | bytes 4915200 | tf_op jit(solution)/shard_map/mul | solution.py:68
  130.6 0.1 broadcast_in_dim.232
  130.7 8.4 %while.34 = (s32[]{:T(128)}, f32[80,640]{1,0:T(8,128)S(1)}, f32[8,80,640]{2,1,0:T(8,128)S(1)}, f32[80]{0:T(128)S(1)}, f32[8,80,640]{2,1,0:T(8,128)}, /*index=5*/s32[]{:T(128)}, s32[]{:T(128)}) while((s32[]{:T(128)}, f32[80,640]{1,0:T(8,128)S(1)}, f32[8,80,640]{2,1,0:T(8,128)S(1)}, f32[80]{0:T(128)S(1)}, f32[8,80,640]{2,1,0:T(8,128)}, ...), condition=%wide.region_3.4_spmd.clone, body=%wide.region_2.3_spmd.clone.sunk | while | flops 153603 | bytes 819803 | solution.py:77
  130.7 1.0 bitcast_dynamic-update-slice_fusion.2
  131.7 1.0 bitcast_dynamic-update-slice_fusion.2
  132.8 1.0 bitcast_dynamic-update-slice_fusion.2
  133.8 1.0 bitcast_dynamic-update-slice_fusion.2
  134.9 1.0 bitcast_dynamic-update-slice_fusion.2
  135.9 1.0 bitcast_dynamic-update-slice_fusion.2
  137.0 1.0 bitcast_dynamic-update-slice_fusion.2
  138.0 1.0 bitcast_dynamic-update-slice_fusion.2
  139.1 0.3 subtract_convert_fusion
  139.4 15.3 %all_to_all.21 = bf16[8,80,640]{2,1,0:T(8,128)(2,1)S(1)} all-to-all(bf16[8,80,640]{2,1,0:T(8,128)(2,1)S(1)} %subtract_convert_fusion), channel_id=1, replica_groups=mesh['tm'=8,'sector'=4] {'tm'}, dimensions={0} | all-to-all | bytes 1638400 | tf_op jit(solution)/shard_map/all_to_all | solution.py:91
  154.6 0.9 copy.35
  (23 shorter events, 0.1 us)
Async XLA Ops:
  6.5 4.5 %copy-start = (bf16[1,640,640]{2,1,0:T(8,128)(2,1)S(1)}, bf16[1,640,640]{2,1,0:T(8,128)(2,1)}, u32[]{:S(2)}) copy-start(bf16[1,640,640]{2,1,0:T(8,128)(2,1)} %param.11) | copy-start | bytes 2457604
  6.5 4.5 %copy-start.1 = (bf16[1,1,640,640]{3,2,1,0:T(8,128)(2,1)S(1)}, bf16[1,1,640,640]{3,2,1,0:T(8,128)(2,1)}, u32[]{:S(2)}) copy-start(bf16[1,1,640,640]{3,2,1,0:T(8,128)(2,1)} %param.10) | copy-start | bytes 2457604
  6.5 65.6 %all-gather.2.cloned.1.call-start = ((), (), s32[]{:S(2)}) async-start(), calls=%async_computation.2 | async-start | bytes 7372800 | tf_op jit(solution)/shard_map/all_gather | solution.py:43
  9.7 23.4 %collective-permute-start.1 = (bf16[1,640,640]{2,1,0:T(8,128)(2,1)}, bf16[1,640,640]{2,1,0:T(8,128)(2,1)S(1)}, u32[]{:S(2)}, u32[]{:S(2)}) collective-permute-start(bf16[1,640,640]{2,1,0:T(8,128)(2,1)} %and_select_fusion.1), channel_id=1, source_target_pairs={{1,0},{2,1},{3,2},{5,4},{6,5},{7,6},{9,8},{10,9},{11,10},{13,12},{... | collective-permute-start | bytes 2457608 | tf_op jit(solution)/shard_map/ppermute | solution.py:10
  13.9 23.4 %collective-permute-start = (bf16[1,640,640]{2,1,0:T(8,128)(2,1)}, bf16[1,640,640]{2,1,0:T(8,128)(2,1)S(1)}, u32[]{:S(2)}, u32[]{:S(2)}) collective-permute-start(bf16[1,640,640]{2,1,0:T(8,128)(2,1)} %fusion.15), channel_id=1, source_target_pairs={{0,1},{1,2},{2,3},{4,5},{5,6},{6,7},{8,9},{9,10},{10,11},{12,13},{... | collective-permute-start | bytes 2457608 | tf_op jit(solution)/shard_map/ppermute | solution.py:10
  33.1 4.2 %copy-start.2 = (bf16[1,640,640]{2,1,0:T(8,128)(2,1)}, bf16[1,640,640]{2,1,0:T(8,128)(2,1)S(1)}, u32[]{:S(2)}) copy-start(bf16[1,640,640]{2,1,0:T(8,128)(2,1)S(1)} %collective-permute-done.1) | copy-start | bytes 2457604
  49.5 17.6 %all-to-all-start = ((bf16[8,2,25600]{2,1,0:T(2,128)(2,1)}), bf16[8,2,25600]{2,1,0:T(2,128)(2,1)}, u32[]{:S(2)}, u32[]{:S(2)}) async-start(bf16[8,2,25600]{2,1,0:T(2,128)(2,1)} %reshape.286), calls=%async_computation | async-start | bytes 1638400 | tf_op jit(solution)/shard_map/all_to_all | solution.py:42
Sparse Core Ops, SparseCore 0:
  9.8 49.5 all-gather.1
where the time goes:
time: 164 us; the launch traced here: 162 us
  other arithmetic  47.3 us (29%)
  waiting for transfers between devices  28.6 us (17%)
  matrix products  24.9 us (15%)
  local copies, waits for them, and re-layouts  19.1 us (12%)
  between operations  15.6 us (10%)
  blocking collectives  15.3 us (9%)
  starting transfers between devices  11.3 us (7%)
    dot_general x4, matrix products, pair_step(): jnp.einsum('uik,ukl->uil', left, window, preferred_element_type=jnp.float32)  18.3 us
    ppermute x2, waiting for transfers between devices, shifted(): return lax.ppermute(block, axis, route)  16.4 us
    all_to_all x1, blocking collectives, per_device(): lax.all_to_all(new_rows, 'tm', split_axis=0, concat_axis=1, tiled=True)  15.3 us
    add x4, other arithmetic, pair_step(): backward + jnp.where((slots < time_count - lag)[:, None, None], product[:...  14.2 us
    concatenate x1, other arithmetic, per_device(): mirrored = jnp.concatenate([history[::-1], history], 0)  12.3 us
    all_to_all x1, waiting for transfers between devices, per_device(): lax.all_to_all(self_energy, 'tm', split_axis=1, concat_axis=0, tiled=True)  12.1 us
    dynamic_update_slice x8, other arithmetic, per_device(): lax.scan(advance, jnp.zeros((rows_each, states), jnp.float32), convolved)  8.25 us
    unnamed x11, local copies, waits for them, and re-layouts  7.55 us
  transfers between devices with their start and end apart: 4, of which 3 were waited for; matrix products, arithmetic and copies ran while one was open for 13% of the time, Pallas kernels for 0%

commit v1 on v0

--- a/solution.py
+++ b/solution.py
@@ -39,7 +39,10 @@
     self_energy = jnp.where(square[None], combined, jnp.zeros((), jnp.float32)).astype(jnp.bfloat16)
     rows_each = states // lax.axis_size("tm")
     first_row = lax.axis_index("tm") * rows_each
-    lag_rows = lax.all_to_all(self_energy, "tm", split_axis=1, concat_axis=0, tiled=True)
+    lag_rows = jnp.concatenate(
+        lax.all_to_all(jnp.stack(jnp.split(self_energy, lax.axis_size("tm"), axis=1)), "tm", 0, 0),
+        axis=0,
+    )
     history = lax.all_gather(masked_prop, "tm", axis=0, tiled=True)
     mirrored = jnp.concatenate([history[::-1], history], 0)
     slots = jnp.arange(time_count, dtype=jnp.int32)

time: 164 us -> 158 us (0.963)
  other arithmetic: 47.3 us -> 41.7 us
  blocking collectives: 15.3 us -> 19.1 us
  local copies, waits for them, and re-layouts: 19.1 us -> 17.3 us
    all_to_all x1, waiting for transfers between devices: 12.1 us -> 0.01 us  [per_device(): lax.all_to_all(jnp.stack(jnp.split(self_energy, lax.axis_size('tm'), axis...]
    all_gather x1, waiting for transfers between devices: 0.01 us -> 11.9 us  [per_device(): history = lax.all_gather(masked_prop, 'tm', axis=0, tiled=True)]
    unnamed x4 -> x3, other arithmetic: 5.64 us -> 0.01 us
    all_to_all x1, blocking collectives: 15.3 us -> 19.1 us  [per_device(): lax.all_to_all(new_rows, 'tm', split_axis=0, concat_axis=1, tiled=True)]
    unnamed x11 -> x14, local copies, waits for them, and re-layouts: 7.55 us -> 6.34 us
  transfers between devices with their start and end apart: 4 -> 4, of which waited for: 3 -> 3; matrix products, arithmetic and copies ran while one was open for 13% -> 20% of each run, Pallas kernels for 0% -> 0%
where the time goes in v1:
time: 158 us; the launch traced here: 157 us
  other arithmetic  41.7 us (26%)
  waiting for transfers between devices  27.3 us (17%)
  matrix products  24.6 us (16%)
  blocking collectives  19.1 us (12%)
  local copies, waits for them, and re-layouts  17.3 us (11%)
  between operations  15.6 us (10%)
  starting transfers between devices  11.1 us (7%)
    all_to_all x1, blocking collectives, per_device(): lax.all_to_all(new_rows, 'tm', split_axis=0, concat_axis=1, tiled=True)  19.1 us
    dot_general x4, matrix products, pair_step(): jnp.einsum('uik,ukl->uil', left, window, preferred_element_type=jnp.float32)  18.3 us
    ppermute x2, waiting for transfers between devices, shifted(): return lax.ppermute(block, axis, route)  15.4 us
    add x4, other arithmetic, pair_step(): backward + jnp.where((slots < time_count - lag)[:, None, None], product[:...  14.1 us
    concatenate x1, other arithmetic, per_device(): mirrored = jnp.concatenate([history[::-1], history], 0)  12.4 us
    all_gather x1, waiting for transfers between devices, per_device(): history = lax.all_gather(masked_prop, 'tm', axis=0, tiled=True)  11.9 us
    dynamic_update_slice x8, other arithmetic, per_device(): lax.scan(advance, jnp.zeros((rows_each, states), jnp.float32), convolved)  8.25 us
    ppermute x2, starting transfers between devices, shifted(): return lax.ppermute(block, axis, route)  6.92 us
  transfers between devices with their start and end apart: 4, of which 3 were waited for; matrix products, arithmetic and copies ran while one was open for 20% of the time, Pallas kernels for 0%

profile of v1, /device:TPU:0, one launch (start us, length us, event | category | flops | bytes accessed | tf_op | source)
XLA Modules:
  0.0 157.0 jit_solution(1185447009855135495)
XLA Ops:
  7.3 2.3 %and_select_fusion.1 = bf16[1,640,640]{2,1,0:T(8,128)(2,1)} fusion(bf16[1,1,640,640]{3,2,1,0:T(8,128)(2,1)} %param.10, pred[640]{0:T(1024)(128)(4,1)S(1)} %iota_compare_fusion.4), kind=kLoop, calls=%fused_computation.23 | loop fusion | flops 819200 | bytes 1639040 | tf_op jit(solution)/shard_map/jit(_where)/select_n | solution.py:21
  9.7 1.3 collective-permute-start.1
  11.0 2.9 %fusion.15 = bf16[1,640,640]{2,1,0:T(8,128)(2,1)} fusion(bf16[1,1,640,640]{3,2,1,0:T(8,128)(2,1)S(1)} %copy-done.1, bf16[1,640,640]{2,1,0:T(8,128)(2,1)S(1)} %copy-done, pred[640]{0:T(1024)(128)(4,1)S(1)} %iota_compare_fusion.4), kind=kOutput, calls=%fused_computation.33 | convolution fusion | flops 1050214400 | bytes 2458240 | tf_op jit(solution)/shard_map/tik,jk->tij/dot_general | solution.py:26
  13.9 5.6 %collective-permute-start = (bf16[1,640,640]{2,1,0:T(8,128)(2,1)}, bf16[1,640,640]{2,1,0:T(8,128)(2,1)S(1)}, u32[]{:S(2)}, u32[]{:S(2)}) collective-permute-start(bf16[1,640,640]{2,1,0:T(8,128)(2,1)} %fusion.15), channel_id=1, source_target_pairs={{0,1},{1,2},{2,3},{4,5},{5,6},{6,7},{8,9},{9,10},{10,11},{12,13},{... | collective-permute-start | bytes 2457608 | tf_op jit(solution)/shard_map/ppermute | solution.py:10
  20.9 0.8 negate_bitcast_fusion
  21.9 11.2 %collective-permute-done.1 = bf16[1,640,640]{2,1,0:T(8,128)(2,1)S(1)} collective-permute-done((bf16[1,640,640]{2,1,0:T(8,128)(2,1)}, bf16[1,640,640]{2,1,0:T(8,128)(2,1)S(1)}, u32[]{:S(2)}, u32[]{:S(2)}) %collective-permute-start.1) | collective-permute-done | bytes 819232 | tf_op jit(solution)/shard_map/ppermute | solution.py:10
  33.1 4.2 %collective-permute-done = bf16[1,640,640]{2,1,0:T(8,128)(2,1)S(1)} collective-permute-done((bf16[1,640,640]{2,1,0:T(8,128)(2,1)}, bf16[1,640,640]{2,1,0:T(8,128)(2,1)S(1)}, u32[]{:S(2)}, u32[]{:S(2)}) %collective-permute-start) | collective-permute-done | bytes 819232 | tf_op jit(solution)/shard_map/ppermute | solution.py:10
  37.3 0.9 copy-done.2
  38.2 3.5 %fusion.13 = bf16[1,640,640]{2,1,0:T(8,128)(2,1)S(1)} fusion(bf16[1,640,640]{2,1,0:T(8,128)(2,1)} %copy-done.2, bf16[1,640,640]{2,1,0:T(8,128)(2,1)S(1)} %collective-permute-done.1, bf16[1,640,640]{2,1,0:T(8,128)(2,1)S(1)} %copy-done, f32[]{:T(128)} %bitcast.94, f32[]{:T(128)} %bitcast.93, pred[640]{0:T(1024)(128)(4,1)S(1)} %iota_compare_fusion.4), kind=kOutput, calls=%fused_computation.24 | convolution fusion | flops 1051852800 | bytes 3277448 | tf_op jit(solution)/shard_map/tik,kl->til/dot_general | solution.py:34
  41.7 0.7 fusion.39
  42.3 0.7 fusion.38
  43.0 0.7 fusion.37
  43.6 0.7 fusion.36
  44.3 0.7 fusion.35
  44.9 0.7 fusion.34
  45.6 0.7 fusion.33
  46.2 0.7 fusion.32
  46.9 4.2 %all-to-all-start = ((bf16[8,1,80,640]{3,2,1,0:T(8,128)(2,1)}), bf16[8,1,80,640]{3,2,1,0:T(8,128)(2,1)}, u32[]{:S(2)}, u32[]{:S(2)}) async-start(bf16[8,1,80,640]{3,2,1,0:T(8,128)(2,1)} %fusion.32), calls=%async_computation | async-start | bytes 1638400 | tf_op jit(solution)/shard_map/all_to_all | solution.py:43
  51.1 11.9 %all-gather.2.cloned.1.call-done = bf16[8,640,640]{2,1,0:T(8,128)(2,1)} async-done(((bf16[1,640,640]{2,1,0:T(8,128)(2,1)}), bf16[8,640,640]{2,1,0:T(8,128)(2,1)}) %all-gather.2.cloned.1.call-update) | async-done | bytes 6553616 | tf_op jit(solution)/shard_map/all_gather | solution.py:46
  63.0 6.3 %rev.6 = bf16[8,640,640]{2,1,0:T(8,128)(2,1)} reverse(bf16[8,640,640]{2,1,0:T(8,128)(2,1)} %all-gather.2.cloned.1.call-done), dimensions={0} | reverse | bytes 13107200 | tf_op jit(solution)/shard_map/rev | solution.py:47
  69.3 12.4 %pad_maximum_fusion = bf16[16,640,640]{2,1,0:T(8,128)(2,1)} fusion(bf16[8,640,640]{2,1,0:T(8,128)(2,1)} %all-gather.2.cloned.1.call-done, bf16[8,640,640]{2,1,0:T(8,128)(2,1)} %rev.6), kind=kLoop, calls=%fused_computation.21 | loop fusion | flops 6553600 | bytes 26214400 | tf_op jit(solution)/shard_map/concatenate | solution.py:47
  81.6 36.4 %while.35 = (s32[]{:T(128)}, f32[8,80,640]{2,1,0:T(8,128)}, f32[8,80,640]{2,1,0:T(8,128)}, bf16[8,80,640]{2,1,0:T(8,128)(2,1)}, bf16[16,640,640]{2,1,0:T(8,128)(...) while((s32[]{:T(128)}, f32[8,80,640]{2,1,0:T(8,128)}, ...), condition=%wide.region_1.2_spmd.clone.clone, body=%wide.region_0.1_spmd.clone.clone.sunk | while | flops 592742400 | bytes 19661552 | solution.py:70
  81.6 1.0 dynamic-slice_bitcast_fusion.3
  82.6 4.6 %fusion.48 = f32[9,80,640]{2,1,0:T(8,128)S(1)} fusion(bf16[16,640,640]{2,1,0:T(8,128)(2,1)} %get-tuple-element.458, s32[]{:T(128)} %get-tuple-element.444, pred[9]{0:T(512)(128)(4,1)S(1)} %iota_compare_fusion.7, bf16[80,640]{1,0:T(8,128)(2,1)S(1)} %get-tuple-element.428, bf16[80,640]{1,0:T(8,128)(2,1)S(1)} %get-tuple-element.429), kind=kOutput, calls=%fused_computation.5.clone.1 | convolution fusion | flops 590284800 | bytes 9421321 | tf_op jit(solution)/shard_map/while/body/eval_jaxpr/uik,ukl->uil/dot_general | solution.py:58
  87.2 2.1 %fusion.49 = (f32[8,80,640]{2,1,0:T(8,128)}, f32[8,80,640]{2,1,0:T(8,128)}) fusion(f32[9,80,640]{2,1,0:T(8,128)S(1)} %fusion.48, f32[8,80,640]{2,1,0:T(8,128)} %get-tuple-element.446, pred[8]{0:T(512)(128)(4,1)S(1)} %get-tuple-element.430, pred[]{:T(512)S(6)} %compare.7, pred[8]{0:T(512)(128)(4,1)S(1)} %get-tuple-element.431, ...), kind=kLoop, calls=%fused_computation.8.clone.1 | loop fusion | flops 2457600 | bytes 9830417 | tf_op jit(solution)/shard_map/while/body/eval_jaxpr/add | solution.py:59
  89.3 1.0 dynamic-slice_bitcast_fusion.3
  90.3 4.6 %fusion.48 = f32[9,80,640]{2,1,0:T(8,128)S(1)} fusion(bf16[16,640,640]{2,1,0:T(8,128)(2,1)} %get-tuple-element.458, s32[]{:T(128)} %get-tuple-element.444, pred[9]{0:T(512)(128)(4,1)S(1)} %iota_compare_fusion.7, bf16[80,640]{1,0:T(8,128)(2,1)S(1)} %get-tuple-element.428, bf16[80,640]{1,0:T(8,128)(2,1)S(1)} %get-tuple-element.429), kind=kOutput, calls=%fused_computation.5.clone.1 | convolution fusion | flops 590284800 | bytes 9421321 | tf_op jit(solution)/shard_map/while/body/eval_jaxpr/uik,ukl->uil/dot_general | solution.py:58
  94.9 4.0 %fusion.49 = (f32[8,80,640]{2,1,0:T(8,128)}, f32[8,80,640]{2,1,0:T(8,128)}) fusion(f32[9,80,640]{2,1,0:T(8,128)S(1)} %fusion.48, f32[8,80,640]{2,1,0:T(8,128)} %get-tuple-element.446, pred[8]{0:T(512)(128)(4,1)S(1)} %get-tuple-element.430, pred[]{:T(512)S(6)} %compare.7, pred[8]{0:T(512)(128)(4,1)S(1)} %get-tuple-element.431, ...), kind=kLoop, calls=%fused_computation.8.clone.1 | loop fusion | flops 2457600 | bytes 9830417 | tf_op jit(solution)/shard_map/while/body/eval_jaxpr/add | solution.py:59
  98.9 1.0 dynamic-slice_bitcast_fusion.3
  99.9 4.6 %fusion.48 = f32[9,80,640]{2,1,0:T(8,128)S(1)} fusion(bf16[16,640,640]{2,1,0:T(8,128)(2,1)} %get-tuple-element.458, s32[]{:T(128)} %get-tuple-element.444, pred[9]{0:T(512)(128)(4,1)S(1)} %iota_compare_fusion.7, bf16[80,640]{1,0:T(8,128)(2,1)S(1)} %get-tuple-element.428, bf16[80,640]{1,0:T(8,128)(2,1)S(1)} %get-tuple-element.429), kind=kOutput, calls=%fused_computation.5.clone.1 | convolution fusion | flops 590284800 | bytes 9421321 | tf_op jit(solution)/shard_map/while/body/eval_jaxpr/uik,ukl->uil/dot_general | solution.py:58
  104.5 4.0 %fusion.49 = (f32[8,80,640]{2,1,0:T(8,128)}, f32[8,80,640]{2,1,0:T(8,128)}) fusion(f32[9,80,640]{2,1,0:T(8,128)S(1)} %fusion.48, f32[8,80,640]{2,1,0:T(8,128)} %get-tuple-element.446, pred[8]{0:T(512)(128)(4,1)S(1)} %get-tuple-element.430, pred[]{:T(512)S(6)} %compare.7, pred[8]{0:T(512)(128)(4,1)S(1)} %get-tuple-element.431, ...), kind=kLoop, calls=%fused_computation.8.clone.1 | loop fusion | flops 2457600 | bytes 9830417 | tf_op jit(solution)/shard_map/while/body/eval_jaxpr/add | solution.py:59
  108.5 1.0 dynamic-slice_bitcast_fusion.3
  109.5 4.6 %fusion.48 = f32[9,80,640]{2,1,0:T(8,128)S(1)} fusion(bf16[16,640,640]{2,1,0:T(8,128)(2,1)} %get-tuple-element.458, s32[]{:T(128)} %get-tuple-element.444, pred[9]{0:T(512)(128)(4,1)S(1)} %iota_compare_fusion.7, bf16[80,640]{1,0:T(8,128)(2,1)S(1)} %get-tuple-element.428, bf16[80,640]{1,0:T(8,128)(2,1)S(1)} %get-tuple-element.429), kind=kOutput, calls=%fused_computation.5.clone.1 | convolution fusion | flops 590284800 | bytes 9421321 | tf_op jit(solution)/shard_map/while/body/eval_jaxpr/uik,ukl->uil/dot_general | solution.py:58
  114.1 4.0 %fusion.49 = (f32[8,80,640]{2,1,0:T(8,128)}, f32[8,80,640]{2,1,0:T(8,128)}) fusion(f32[9,80,640]{2,1,0:T(8,128)S(1)} %fusion.48, f32[8,80,640]{2,1,0:T(8,128)} %get-tuple-element.446, pred[8]{0:T(512)(128)(4,1)S(1)} %get-tuple-element.430, pred[]{:T(512)S(6)} %compare.7, pred[8]{0:T(512)(128)(4,1)S(1)} %get-tuple-element.431, ...), kind=kLoop, calls=%fused_computation.8.clone.1 | loop fusion | flops 2457600 | bytes 9830417 | tf_op jit(solution)/shard_map/while/body/eval_jaxpr/add | solution.py:59
  118.1 3.3 %add_multiply_fusion = f32[8,80,640]{2,1,0:T(8,128)} fusion(f32[8,80,640]{2,1,0:T(8,128)} %get-tuple-element.265, f32[8,80,640]{2,1,0:T(8,128)} %get-tuple-element.266), kind=kLoop, calls=%fused_computation.27 | loop fusion | flops 819200 | bytes 4915200 | tf_op jit(solution)/shard_map/mul | solution.py:71
  121.4 0.1 broadcast_in_dim.232
  121.5 8.4 %while.34 = (s32[]{:T(128)}, f32[80,640]{1,0:T(8,128)S(1)}, f32[8,80,640]{2,1,0:T(8,128)S(1)}, f32[80]{0:T(128)S(1)}, f32[8,80,640]{2,1,0:T(8,128)}, /*index=5*/s32[]{:T(128)}, s32[]{:T(128)}) while((s32[]{:T(128)}, f32[80,640]{1,0:T(8,128)S(1)}, f32[8,80,640]{2,1,0:T(8,128)S(1)}, f32[80]{0:T(128)S(1)}, f32[8,80,640]{2,1,0:T(8,128)}, ...), condition=%wide.region_3.4_spmd.clone, body=%wide.region_2.3_spmd.clone.sunk | while | flops 153603 | bytes 819803 | solution.py:80
  121.5 1.0 bitcast_dynamic-update-slice_fusion.2
  122.5 1.0 bitcast_dynamic-update-slice_fusion.2
  123.6 1.0 bitcast_dynamic-update-slice_fusion.2
  124.6 1.0 bitcast_dynamic-update-slice_fusion.2
  125.7 1.0 bitcast_dynamic-update-slice_fusion.2
  126.7 1.0 bitcast_dynamic-update-slice_fusion.2
  127.8 1.0 bitcast_dynamic-update-slice_fusion.2
  128.8 1.0 bitcast_dynamic-update-slice_fusion.2
  129.9 0.3 subtract_convert_fusion
  130.2 19.1 %all_to_all.14 = bf16[8,80,640]{2,1,0:T(8,128)(2,1)S(1)} all-to-all(bf16[8,80,640]{2,1,0:T(8,128)(2,1)S(1)} %subtract_convert_fusion), channel_id=1, replica_groups=mesh['tm'=8,'sector'=4] {'tm'}, dimensions={0} | all-to-all | bytes 1638400 | tf_op jit(solution)/shard_map/all_to_all | solution.py:94
  149.3 0.9 copy.37
  (25 shorter events, 0.3 us)
Async XLA Ops:
  6.5 4.5 %copy-start = (bf16[1,640,640]{2,1,0:T(8,128)(2,1)S(1)}, bf16[1,640,640]{2,1,0:T(8,128)(2,1)}, u32[]{:S(2)}) copy-start(bf16[1,640,640]{2,1,0:T(8,128)(2,1)} %param.11) | copy-start | bytes 2457604
  6.5 4.5 %copy-start.1 = (bf16[1,1,640,640]{3,2,1,0:T(8,128)(2,1)S(1)}, bf16[1,1,640,640]{3,2,1,0:T(8,128)(2,1)}, u32[]{:S(2)}) copy-start(bf16[1,1,640,640]{3,2,1,0:T(8,128)(2,1)} %param.10) | copy-start | bytes 2457604
  6.5 56.4 %all-gather.2.cloned.1.call-start = ((), (), s32[]{:S(2)}) async-start(), calls=%async_computation.2 | async-start | bytes 7372800 | tf_op jit(solution)/shard_map/all_gather | solution.py:46
  9.7 23.4 %collective-permute-start.1 = (bf16[1,640,640]{2,1,0:T(8,128)(2,1)}, bf16[1,640,640]{2,1,0:T(8,128)(2,1)S(1)}, u32[]{:S(2)}, u32[]{:S(2)}) collective-permute-start(bf16[1,640,640]{2,1,0:T(8,128)(2,1)} %and_select_fusion.1), channel_id=1, source_target_pairs={{1,0},{2,1},{3,2},{5,4},{6,5},{7,6},{9,8},{10,9},{11,10},{13,12},{... | collective-permute-start | bytes 2457608 | tf_op jit(solution)/shard_map/ppermute | solution.py:10
  13.9 23.4 %collective-permute-start = (bf16[1,640,640]{2,1,0:T(8,128)(2,1)}, bf16[1,640,640]{2,1,0:T(8,128)(2,1)S(1)}, u32[]{:S(2)}, u32[]{:S(2)}) collective-permute-start(bf16[1,640,640]{2,1,0:T(8,128)(2,1)} %fusion.15), channel_id=1, source_target_pairs={{0,1},{1,2},{2,3},{4,5},{5,6},{6,7},{8,9},{9,10},{10,11},{12,13},{... | collective-permute-start | bytes 2457608 | tf_op jit(solution)/shard_map/ppermute | solution.py:10
  37.3 0.9 copy-start.2
  46.9 34.8 %all-to-all-start = ((bf16[8,1,80,640]{3,2,1,0:T(8,128)(2,1)}), bf16[8,1,80,640]{3,2,1,0:T(8,128)(2,1)}, u32[]{:S(2)}, u32[]{:S(2)}) async-start(bf16[8,1,80,640]{3,2,1,0:T(8,128)(2,1)} %fusion.32), calls=%async_computation | async-start | bytes 1638400 | tf_op jit(solution)/shard_map/all_to_all | solution.py:43
Sparse Core Ops, SparseCore 0:
  9.8 53.0 all-gather.1
